TPU v7x, 32 devices: a whole 2x2x4 slice. The times are simulated.
32 devices in a mesh: seg: 2 (over x), rows: 16 (over z, y, core).
Axes of the slice: x: 2, y: 2, z: 4, core: 2. Of those that a mesh axis runs over, the one named last changes fastest.
Arguments:
- snapshots: float32 [512, 131072], P('seg', 'rows'), parts along dimension 0, may hold values from -400 to 400
Outputs:
- q_panel: float32 [64, 131072], P('seg', 'rows'), parts along dimension 0
- r_panel: float32 [64, 32], P('seg'), parts along dimension 0
- projected: float32 [64, 224], P('seg'), parts along dimension 0
- trailing: float32 [448, 131072], P('seg', 'rows'), parts along dimension 0
There are 2 independent parts, one for each index of `seg`. A program takes and returns all parts, laid end to end along the dimension named above; each array names one. Nothing has to cross between parts.
All inputs are finite; a program needn't handle non-finite values.
Results may differ from a plain program's by a relative error of at most 0.000082.
Values sent between devices are 32-bit elements; how exact they have to be, the bound alone decides.
A program may use at most 64 MiB of HBM per device.

v0:
```python
import jax
import jax.numpy as jnp
from jax import lax
from jax.sharding import PartitionSpec as P

PANEL = 32


def inner(left, right):
    return lax.dot_general(
        left,
        right,
        (((1,), (1,)), ((), ())),
        precision=lax.Precision.HIGHEST,
        preferred_element_type=jnp.float32,
    )


def local(snapshots):
    panel = snapshots[:PANEL]
    rest = snapshots[PANEL:]
    totals = lax.psum(inner(panel, snapshots), "rows")
    lower = jnp.linalg.cholesky(totals[:, :PANEL])
    q_panel = jax.scipy.linalg.solve_triangular(lower, panel, lower=True)
    projected = jax.scipy.linalg.solve_triangular(lower, totals[:, PANEL:], lower=True)
    update = lax.dot_general(
        projected,
        q_panel,
        (((0,), (0,)), ((), ())),
        precision=lax.Precision.HIGHEST,
        preferred_element_type=jnp.float32,
    )
    trailing = rest - update
    return (q_panel, lower.T, projected, trailing)


def solution(mesh):
    return jax.shard_map(
        local,
        mesh=mesh,
        in_specs=(P("seg", "rows"),),
        out_specs=(P("seg", "rows"), P("seg", None), P("seg", None), P("seg", "rows")),
        check_vma=False,
    )
```

profile of v0, /device:TPU:0, one launch (start us, length us, event | category | flops | bytes accessed | tf_op | source)
XLA Modules:
  0.0 94.1 jit_solution(7879214852546602777)
XLA Ops:
  0.6 9.2 %fusion.2 = f32[32,256]{0,1:T(8,128)S(1)} fusion(f32[256,8192]{1,0:T(8,128)} %param.1), kind=kOutput, calls=%fused_computation.3 | convolution fusion | flops 805306368 | bytes 9469952 | tf_op jit(solution)/shard_map/dot_general | solution.py:10
  9.8 63.8 %psum.7 = f32[32,256]{0,1:T(8,128)S(1)} all-reduce(f32[32,256]{0,1:T(8,128)S(1)} %fusion.2), channel_id=1, replica_groups=mesh['seg'=2,'rows'=16] {'rows'}, use_global_device_ids=true, to_apply=%region_0.0 | all-reduce | flops 8192 | bytes 65536 | tf_op jit(solution)/shard_map/psum | solution.py:22
  73.6 0.1 copy.6
  73.7 2.9 %cholesky.16 = f32[32,32]{1,0:T(8,128)S(1)} custom-call(f32[32,32]{1,0:T(8,128)S(1)} %fusion.8), custom_call_target="Cholesky" | custom-call | tf_op jit(solution)/shard_map/jit(cholesky)/cholesky | solution.py:23
  76.6 0.6 compare_reduce_fusion
  77.3 0.7 fusion.9
  78.0 0.7 copy.7
  78.6 2.4 %custom-call.10 = f32[1,32,32]{1,2,0:T(8,128)S(1)} custom-call(f32[1,32,32]{2,1,0:T(8,128)S(1)} %get-tuple-element.9), custom_call_target="InvertDiagBlocksLowerTriangular" | custom-call | tf_op jit(solution)/shard_map/jit(_solve_triangular)/triangular_solve | solution.py:24
  81.1 0.4 fusion.4
  81.4 0.0 copy-start.1
  81.4 2.3 %fusion = f32[32,8192]{1,0:T(8,128)S(1)} fusion(f32[256,8192]{1,0:T(8,128)} %param.1, f32[1,32,32]{1,2,0:T(8,128)S(1)} %custom-call.10), kind=kOutput, calls=%fused_computation.1 | convolution fusion | flops 100663296 | bytes 2101248 | tf_op jit(solution)/shard_map/jit(_solve_triangular)/triangular_solve | solution.py:24
  83.7 0.0 copy-start
  83.7 10.4 %convolution_subtract_fusion = f32[224,8192]{1,0:T(8,128)} fusion(f32[32,224]{1,0:T(8,128)S(1)} %fusion.4, f32[32,8192]{1,0:T(8,128)S(1)} %fusion, f32[256,8192]{1,0:T(8,128)} %param.1), kind=kOutput, calls=%fused_computation | convolution fusion | flops 706478080 | bytes 15757312 | tf_op jit(solution)/shard_map/dot_general | solution.py:26
  94.1 0.0 copy-done.1
  94.1 0.0 copy-done
  (3 shorter events, 0.0 us)
Async XLA Ops:
  81.4 12.7 %copy-start.1 = (f32[32,224]{1,0:T(8,128)}, f32[32,224]{1,0:T(8,128)S(1)}, u32[]{:S(2)}) copy-start(f32[32,224]{1,0:T(8,128)S(1)} %fusion.4) | copy-start | bytes 86020
  83.7 10.4 %copy-start = (f32[32,8192]{1,0:T(8,128)}, f32[32,8192]{1,0:T(8,128)S(1)}, u32[]{:S(2)}) copy-start(f32[32,8192]{1,0:T(8,128)S(1)} %fusion) | copy-start | bytes 3145732
where the time goes:
time: 94.3 us; the launch traced here: 94.1 us
  blocking collectives  63.8 us (68%)
  matrix products  22.2 us (24%)
  other arithmetic  6.69 us (7%)
    psum x1, blocking collectives, local(): totals = lax.psum(inner(panel, snapshots), 'rows')  63.8 us
    dot_general x1, matrix products, local(): lax.dot_general(projected, q_panel, (((0,), (0,)), ((), ())), precision=l...  10.4 us
    dot_general x1, matrix products, inner(): lax.dot_general(left, right, (((1,), (1,)), ((), ())), precision=lax.Prec...  9.17 us
    another operation x3, other arithmetic, local(): lower = jnp.linalg.cholesky(totals[:, :PANEL])  3.6 us
    another operation x1, other arithmetic, local(): q_panel = jax.scipy.linalg.solve_triangular(lower, panel, lower=True)  2.44 us
    another operation x1, matrix products, local(): q_panel = jax.scipy.linalg.solve_triangular(lower, panel, lower=True)  2.26 us

commit v1 on v0

v1 whole, which is shorter than its diff:
```python
import functools

import jax
import jax.numpy as jnp
from jax import lax
from jax.experimental import pallas as pl
from jax.experimental.pallas import tpu as pltpu
from jax.sharding import PartitionSpec as P

PANEL = 32
CHUNK = 1024
MESH = pl.DeviceIdType.MESH


def split(value):
    high = value.astype(jnp.bfloat16)
    return high, (value - high.astype(jnp.float32)).astype(jnp.bfloat16)


def reduce_kernel(chips, x_hbm, snap, stack, total, acc, part, pair_in, slots, full,
                  load_sem, pair_send, pair_recv, chip_send, chip_recv, last_send, last_recv):
    me = lax.axis_index("rows")
    core = lax.rem(me, 2)
    chip = lax.div(me, 2)
    partner = me + 1 - 2 * core
    cols, width = snap.shape
    chunks = width // CHUNK

    def load(c):
        where = pl.ds(pl.multiple_of(c * CHUNK, CHUNK), CHUNK)
        return pltpu.make_async_copy(x_hbm.at[:, where], snap.at[:, where], load_sem.at[c])

    for c in range(chunks):
        load(c).start()

    barrier = pltpu.get_barrier_semaphore()
    pl.semaphore_signal(barrier, inc=1, device_id={"rows": partner}, device_id_type=MESH)
    for k in range(1, chips):
        peer = lax.rem(chip + k, chips) * 2 + core
        pl.semaphore_signal(barrier, inc=1, device_id={"rows": peer}, device_id_type=MESH)

    acc[...] = jnp.zeros_like(acc)
    for c in range(chunks):
        load(c).wait()
        where = pl.ds(c * CHUNK, CHUNK)
        high, low = split(snap[:, where])
        panel = jnp.concatenate([high[:PANEL], low[:PANEL]], axis=0)
        stack[:, where] = panel
        acc[...] += lax.dot_general(
            jnp.concatenate([high, low], axis=0), panel, (((1,), (1,)), ((), ())),
            preferred_element_type=jnp.float32)
    both = acc[:cols] + acc[cols:]
    gram = (both[:, :PANEL] + both[:, PANEL:]).T
    half = PANEL // 2
    part[0] = gram[:half]
    part[1] = gram[half:]

    pl.semaphore_wait(barrier, chips)
    pair = pltpu.make_async_remote_copy(
        src_ref=part.at[1 - core], dst_ref=pair_in, send_sem=pair_send, recv_sem=pair_recv,
        device_id={"rows": partner}, device_id_type=MESH)
    pair.start()
    pair.wait()
    slots[chip] = part[core] + pair_in[...]

    def send(k):
        peer = lax.rem(chip + k, chips) * 2 + core
        return pltpu.make_async_remote_copy(
            src_ref=slots.at[chip], dst_ref=slots.at[chip], send_sem=chip_send.at[k - 1],
            recv_sem=chip_recv.at[k - 1], device_id={"rows": peer}, device_id_type=MESH)

    for k in range(1, chips):
        send(k).start()
    for k in range(1, chips):
        send(k).wait_recv()
    whole = slots[0]
    for k in range(1, chips):
        whole = whole + slots[k]
    full[core] = whole
    last = pltpu.make_async_remote_copy(
        src_ref=full.at[core], dst_ref=full.at[core], send_sem=last_send, recv_sem=last_recv,
        device_id={"rows": partner}, device_id_type=MESH)
    last.start()
    for k in range(1, chips):
        send(k).wait_send()
    last.wait()
    total[...] = full[...]


def update_kernel(snap, stack, total, q_ref, r_ref, projected_ref, trailing_ref, coef):
    step = pl.program_id(0)
    cols = snap.shape[0]

    @pl.when(step == 0)
    def _():
        a = total[...].reshape(PANEL, cols)
        rows = lax.broadcasted_iota(jnp.int32, (PANEL, 1), 0)
        eye = jnp.where(rows == lax.broadcasted_iota(jnp.int32, (PANEL, PANEL), 1), 1.0, 0.0)
        inv = eye
        upper, lower = jnp.zeros_like(a), jnp.zeros_like(inv)
        pivots = jnp.zeros((PANEL, 1), jnp.float32)
        for j in range(PANEL):
            at = rows == j
            pivot = a[j:j + 1, j:j + 1]
            upper = jnp.where(at, a, upper)
            lower = jnp.where(at, inv, lower)
            pivots = jnp.where(at, pivot, pivots)
            column = a[:, j:j + 1]
            recip = 1.0 / pivot
            a_row, inv_row = a[j:j + 1] * recip, inv[j:j + 1] * recip
            a = jnp.where(at, a_row, a - column * a_row)
            inv = jnp.where(at, inv_row, inv - column * inv_row)
        scale = 1.0 / jnp.sqrt(pivots)
        upper, lower = upper * scale, lower * scale
        lanes = lax.broadcasted_iota(jnp.int32, (PANEL, PANEL), 1)
        r_ref[...] = jnp.where(lanes >= rows, upper[:, :PANEL], 0.0)
        projected_ref[...] = upper[:, PANEL:]
        lower = jnp.where(lanes <= rows, lower, 0.0)
        weights = jnp.concatenate([lower, -(a.T)[PANEL:]], axis=0)
        high, low = split(weights)
        coef[...] = jnp.concatenate([high, high, low, low], axis=1)

    where = pl.ds(pl.multiple_of(step * CHUNK, CHUNK), CHUNK)
    panel = stack[:, where]
    out = lax.dot_general(
        coef[...], jnp.concatenate([panel, panel], axis=0), (((1,), (0,)), ((), ())),
        preferred_element_type=jnp.float32)
    q_ref[...] = out[:PANEL]
    trailing_ref[...] = snap[PANEL:, where] + out[PANEL:]


def local(rows, snapshots):
    cols, width = snapshots.shape
    chips = rows // 2
    half = PANEL // 2
    f32 = jnp.float32
    vmem = pl.BlockSpec(memory_space=pltpu.VMEM)
    snap, stack, total = pl.pallas_call(
        functools.partial(reduce_kernel, chips),
        out_shape=(
            pltpu.VMEM((cols, width), f32),
            pltpu.VMEM((2 * PANEL, width), jnp.bfloat16),
            pltpu.VMEM((2, half, cols), f32)),
        in_specs=[pl.BlockSpec(memory_space=pltpu.HBM)],
        out_specs=(vmem, vmem, vmem),
        scratch_shapes=[
            pltpu.VMEM((2 * cols, 2 * PANEL), f32),
            pltpu.VMEM((2, half, cols), f32),
            pltpu.VMEM((half, cols), f32),
            pltpu.VMEM((chips, half, cols), f32),
            pltpu.VMEM((2, half, cols), f32),
            pltpu.SemaphoreType.DMA((width // CHUNK,)),
            pltpu.SemaphoreType.DMA,
            pltpu.SemaphoreType.DMA,
            pltpu.SemaphoreType.DMA((chips - 1,)),
            pltpu.SemaphoreType.DMA((chips - 1,)),
            pltpu.SemaphoreType.DMA,
            pltpu.SemaphoreType.DMA,
        ],
        compiler_params=pltpu.CompilerParams(
            collective_id=0, has_side_effects=True, vmem_limit_bytes=24 << 20),
        name="reduce",
    )(snapshots)
    return pl.pallas_call(
        update_kernel,
        grid=(width // CHUNK,),
        out_shape=(
            jax.ShapeDtypeStruct((PANEL, width), f32),
            jax.ShapeDtypeStruct((PANEL, PANEL), f32),
            jax.ShapeDtypeStruct((PANEL, cols - PANEL), f32),
            jax.ShapeDtypeStruct((cols - PANEL, width), f32)),
        in_specs=[vmem, vmem, vmem],
        out_specs=(
            pl.BlockSpec((PANEL, CHUNK), lambda i: (0, i)),
            pl.BlockSpec((PANEL, PANEL), lambda i: (0, 0)),
            pl.BlockSpec((PANEL, cols - PANEL), lambda i: (0, 0)),
            pl.BlockSpec((cols - PANEL, CHUNK), lambda i: (0, i))),
        scratch_shapes=[pltpu.VMEM((cols, 4 * PANEL), jnp.bfloat16)],
        compiler_params=pltpu.CompilerParams(
            dimension_semantics=("arbitrary",), vmem_limit_bytes=24 << 20),
        name="update",
    )(snap, stack, total)


def solution(mesh):
    return jax.shard_map(
        functools.partial(local, mesh.shape["rows"]),
        mesh=mesh,
        in_specs=(P("seg", "rows"),),
        out_specs=(P("seg", "rows"), P("seg", None), P("seg", None), P("seg", "rows")),
        check_vma=False,
    )
```

time: 94.3 us -> 27.1 us (0.29)
  blocking collectives: 63.8 us -> 0 us
  Pallas kernels: 0 us -> 23 us
  matrix products: 22.2 us -> 0 us
  other arithmetic: 6.69 us -> 0 us
  local copies, waits for them, and re-layouts: 0.77 us -> 3.37 us
    psum x1 -> x0, blocking collectives: 63.8 us -> none  [local(): totals = lax.psum(inner(panel, snapshots), 'rows')]
    pallas_call x0 -> x2, Pallas kernels: none -> 23 us  [the longest x1 14.5 us: local(): pl.pallas_call(functools.partial(reduce_kernel, chips), out_shape=(pltpu....]
    dot_general x2 -> x0, matrix products: 19.6 us -> none  [the longest x1 10.4 us: local(): lax.dot_general(projected, q_panel, (((0,), (0,)), ((), ())), precision=l...]
    another operation x4 -> x0, other arithmetic: 6.03 us -> none  [the longest x3 3.6 us: local(): lower = jnp.linalg.cholesky(totals[:, :PANEL])]
    unnamed x5 -> x2, local copies, waits for them, and re-layouts: 0.69 us -> 3.37 us
    another operation x2 -> x0, matrix products: 2.61 us -> none  [the longest x1 2.26 us: local(): q_panel = jax.scipy.linalg.solve_triangular(lower, panel, lower=True)]
where the time goes in v1:
time: 27.1 us; the launch traced here: 27 us
  Pallas kernels  23 us (85%)
  local copies, waits for them, and re-layouts  3.37 us (12%)
  between operations  0.65 us (2%)
    pallas_call x1, Pallas kernels, local(): pl.pallas_call(functools.partial(reduce_kernel, chips), out_shape=(pltpu....  14.5 us
    pallas_call x1, Pallas kernels, local(): pl.pallas_call(update_kernel, grid=(width // CHUNK,), out_shape=(jax.Shap...  8.44 us
    unnamed x2, local copies, waits for them, and re-layouts  3.37 us

profile of v1, /device:TPU:0, one launch (start us, length us, event | category | flops | bytes accessed | tf_op | source)
XLA Modules:
  0.0 27.0 jit_solution(9829599527226611442)
XLA Ops:
  0.6 0.0 copy-start
  0.6 3.4 %copy-done = f32[256,8192]{1,0:T(8,128)S(1)} copy-done((f32[256,8192]{1,0:T(8,128)S(1)}, f32[256,8192]{1,0:T(8,128)}, u32[]{:S(2)}) %copy-start) | copy-done | bytes 8388632
  4.0 14.5 %reduce.1 = (f32[256,8192]{1,0:T(8,128)S(1)}, bf16[64,8192]{1,0:T(8,128)(2,1)S(1)}, f32[2,16,256]{2,1,0:T(8,128)S(1)}) custom-call(f32[256,8192]{1,0:T(8,128)S(1)} %copy-done), custom_call_target="tpu_custom_call" | custom-call | tf_op jit(solution)/shard_map/reduce/pallas_call | solution.py:138
  18.5 8.4 %update.1 = (f32[32,8192]{1,0:T(8,128)}, f32[32,32]{1,0:T(8,128)}, f32[32,224]{1,0:T(8,128)}, f32[224,8192]{1,0:T(8,128)}) custom-call(f32[256,8192]{1,0:T(8,128)S(1)} %get-tuple-element.7.snap, bf16[64,8192]{1,0:T(8,128)(2,1)S(1)} %get-tuple-element.8.stack, f32[2,16,256]{2,1,0:T(8,128)S(1)} %get-tuple-element.9.total), custom_call_target="tpu_custom_call" | custom-call | tf_op jit(solution)/shard_map/update/pallas_call | solution.py:164
Async XLA Ops:
  0.6 3.4 %copy-start = (f32[256,8192]{1,0:T(8,128)S(1)}, f32[256,8192]{1,0:T(8,128)}, u32[]{:S(2)}) copy-start(f32[256,8192]{1,0:T(8,128)} %x_hbm.1) | copy-start | bytes 25165828

commit v2 on v1

--- a/solution.py
+++ b/solution.py
@@ -9,6 +9,8 @@
 
 PANEL = 32
 CHUNK = 1024
+LANES = 128
+BLOCK = 8
 MESH = pl.DeviceIdType.MESH
 
 
@@ -87,46 +89,77 @@
     total[...] = full[...]
 
 
-def update_kernel(snap, stack, total, q_ref, r_ref, projected_ref, trailing_ref, coef):
-    step = pl.program_id(0)
-    cols = snap.shape[0]
-
-    @pl.when(step == 0)
-    def _():
-        a = total[...].reshape(PANEL, cols)
-        rows = lax.broadcasted_iota(jnp.int32, (PANEL, 1), 0)
-        eye = jnp.where(rows == lax.broadcasted_iota(jnp.int32, (PANEL, PANEL), 1), 1.0, 0.0)
-        inv = eye
-        upper, lower = jnp.zeros_like(a), jnp.zeros_like(inv)
-        pivots = jnp.zeros((PANEL, 1), jnp.float32)
-        for j in range(PANEL):
-            at = rows == j
-            pivot = a[j:j + 1, j:j + 1]
-            upper = jnp.where(at, a, upper)
-            lower = jnp.where(at, inv, lower)
-            pivots = jnp.where(at, pivot, pivots)
-            column = a[:, j:j + 1]
+def eliminate(total, tiles):
+    groups = PANEL // 8
+    rows = lax.broadcasted_iota(jnp.int32, (8, LANES), 0)
+    lanes = lax.broadcasted_iota(jnp.int32, (8, LANES), 1)
+    a = [[total[8 * g:8 * g + 8, LANES * t:LANES * (t + 1)] for g in range(groups)] for t in range(tiles)]
+    a.append([jnp.where(lanes == rows + 8 * g, 1.0, 0.0) for g in range(groups)])
+    kept = [[None] * groups for _ in a]
+    pivots = [None] * groups
+    for start in range(0, PANEL, BLOCK):
+        columns = [
+            [jnp.broadcast_to(block[:, j:j + 1], (8, LANES)) for block in a[0]]
+            for j in range(start, start + BLOCK)]
+        for k in range(BLOCK):
+            j = start + k
+            group, at = j // 8, rows == j % 8
+            column = columns[k]
+            pivot = column[group][j % 8:j % 8 + 1]
             recip = 1.0 / pivot
-            a_row, inv_row = a[j:j + 1] * recip, inv[j:j + 1] * recip
-            a = jnp.where(at, a_row, a - column * a_row)
-            inv = jnp.where(at, inv_row, inv - column * inv_row)
-        scale = 1.0 / jnp.sqrt(pivots)
-        upper, lower = upper * scale, lower * scale
-        lanes = lax.broadcasted_iota(jnp.int32, (PANEL, PANEL), 1)
-        r_ref[...] = jnp.where(lanes >= rows, upper[:, :PANEL], 0.0)
-        projected_ref[...] = upper[:, PANEL:]
-        lower = jnp.where(lanes <= rows, lower, 0.0)
-        weights = jnp.concatenate([lower, -(a.T)[PANEL:]], axis=0)
-        high, low = split(weights)
-        coef[...] = jnp.concatenate([high, high, low, low], axis=1)
-
-    where = pl.ds(pl.multiple_of(step * CHUNK, CHUNK), CHUNK)
-    panel = stack[:, where]
-    out = lax.dot_general(
-        coef[...], jnp.concatenate([panel, panel], axis=0), (((1,), (0,)), ((), ())),
-        preferred_element_type=jnp.float32)
-    q_ref[...] = out[:PANEL]
-    trailing_ref[...] = snap[PANEL:, where] + out[PANEL:]
+
+            def step(blocks):
+                row = blocks[group][j % 8:j % 8 + 1] * recip
+                updated = [block - scale * row for block, scale in zip(blocks, column)]
+                updated[group] = jnp.where(at, row, updated[group])
+                return updated
+
+            for t in range(len(a)):
+                old = a[t][group]
+                kept[t][group] = old if j % 8 == 0 else jnp.where(at, old, kept[t][group])
+            pivots[group] = pivot if j % 8 == 0 else jnp.where(at, pivot, pivots[group])
+            columns[k + 1:] = [step(blocks) for blocks in columns[k + 1:]]
+            a = [step(blocks) for blocks in a]
+    for g in range(groups):
+        scale = 1.0 / jnp.sqrt(pivots[g])
+        for t in range(len(a)):
+            kept[t][g] = kept[t][g] * scale
+        kept[0][g] = jnp.where((lanes >= rows + 8 * g) | (lanes >= PANEL), kept[0][g], 0.0)
+        kept[tiles][g] = jnp.where(lanes <= rows + 8 * g, kept[tiles][g], 0.0)
+    join = lambda blocks: jnp.concatenate(blocks, axis=0)
+    solved = jnp.concatenate([join(a[t]) for t in range(tiles)], axis=1)
+    upper = jnp.concatenate([join(kept[t]) for t in range(tiles)], axis=1)
+    return upper, join(kept[tiles])[:, :PANEL], solved
+
+
+def update_kernel(snap, stack, total, q_ref, r_ref, projected_ref, trailing_ref,
+                  out, r_buf, projected_buf, sems):
+    cols, width = snap.shape
+    upper, lower, solved = eliminate(total[...].reshape(PANEL, cols), cols // LANES)
+    r_buf[...] = upper[:, :PANEL]
+    projected_buf[...] = upper[:, PANEL:]
+    copies = [
+        pltpu.make_async_copy(r_buf, r_ref, sems.at[0]),
+        pltpu.make_async_copy(projected_buf, projected_ref, sems.at[1])]
+    for copy in copies:
+        copy.start()
+    weights = jnp.concatenate([lower, -(solved.T)[PANEL:]], axis=0)
+    high, low = split(weights)
+    coef = jnp.concatenate([high, high, low, low], axis=1)
+    for c in range(width // CHUNK):
+        where = pl.ds(c * CHUNK, CHUNK)
+        panel = stack[:, where]
+        delta = lax.dot_general(
+            coef, jnp.concatenate([panel, panel], axis=0), (((1,), (0,)), ((), ())),
+            preferred_element_type=jnp.float32)
+        out[:PANEL, where] = delta[:PANEL]
+        out[PANEL:, where] = snap[PANEL:, where] + delta[PANEL:]
+        for ref, rows, sem in ((q_ref, pl.ds(0, PANEL), 2 * c + 2), (trailing_ref, pl.ds(PANEL, cols - PANEL), 2 * c + 3)):
+            copy = pltpu.make_async_copy(out.at[rows, where], ref.at[:, where], sems.at[sem])
+            copy.start()
+            copies.append(copy)
+    for copy in copies:
+        copy.wait()
 
 
 def local(rows, snapshots):
@@ -158,26 +191,25 @@
             pltpu.SemaphoreType.DMA,
         ],
         compiler_params=pltpu.CompilerParams(
-            collective_id=0, has_side_effects=True, vmem_limit_bytes=24 << 20),
+            collective_id=0, has_side_effects=True, vmem_limit_bytes=50 << 20),
         name="reduce",
     )(snapshots)
     return pl.pallas_call(
         update_kernel,
-        grid=(width // CHUNK,),
         out_shape=(
             jax.ShapeDtypeStruct((PANEL, width), f32),
             jax.ShapeDtypeStruct((PANEL, PANEL), f32),
             jax.ShapeDtypeStruct((PANEL, cols - PANEL), f32),
             jax.ShapeDtypeStruct((cols - PANEL, width), f32)),
         in_specs=[vmem, vmem, vmem],
-        out_specs=(
-            pl.BlockSpec((PANEL, CHUNK), lambda i: (0, i)),
-            pl.BlockSpec((PANEL, PANEL), lambda i: (0, 0)),
-            pl.BlockSpec((PANEL, cols - PANEL), lambda i: (0, 0)),
-            pl.BlockSpec((cols - PANEL, CHUNK), lambda i: (0, i))),
-        scratch_shapes=[pltpu.VMEM((cols, 4 * PANEL), jnp.bfloat16)],
-        compiler_params=pltpu.CompilerParams(
-            dimension_semantics=("arbitrary",), vmem_limit_bytes=24 << 20),
+        out_specs=(pl.BlockSpec(memory_space=pltpu.HBM),) * 4,
+        scratch_shapes=[
+            pltpu.VMEM((cols, width), f32),
+            pltpu.VMEM((PANEL, PANEL), f32),
+            pltpu.VMEM((PANEL, cols - PANEL), f32),
+            pltpu.SemaphoreType.DMA((2 * (width // CHUNK) + 2,)),
+        ],
+        compiler_params=pltpu.CompilerParams(vmem_limit_bytes=32 << 20),
         name="update",
     )(snap, stack, total)
 

time: 27.1 us -> 20.3 us (0.75)
  Pallas kernels: 23 us -> 19.5 us
  local copies, waits for them, and re-layouts: 3.37 us -> 0 us
    pallas_call x1, Pallas kernels: 8.44 us -> 4.7 us  [local(): pl.pallas_call(update_kernel, out_shape=(jax.ShapeDtypeStruct((PANEL, wid...]
    unnamed x2 -> x0, local copies, waits for them, and re-layouts: 3.37 us -> none
where the time goes in v2:
time: 20.3 us; the launch traced here: 20.1 us
  Pallas kernels  19.5 us (96%)
  between operations  0.64 us (3%)
    pallas_call x1, Pallas kernels, local(): pl.pallas_call(functools.partial(reduce_kernel, chips), out_shape=(pltpu....  14.8 us
    pallas_call x1, Pallas kernels, local(): pl.pallas_call(update_kernel, out_shape=(jax.ShapeDtypeStruct((PANEL, wid...  4.7 us

profile of v2, /device:TPU:0, one launch (start us, length us, event | category | flops | bytes accessed | tf_op | source)
XLA Modules:
  0.0 20.1 jit_solution(9261411445263298765)
XLA Ops:
  0.6 14.8 %reduce.1 = (f32[256,8192]{1,0:T(8,128)S(1)}, bf16[64,8192]{1,0:T(8,128)(2,1)S(1)}, f32[2,16,256]{2,1,0:T(8,128)S(1)}) custom-call(f32[256,8192]{1,0:T(8,128)} %x_hbm.1), custom_call_target="tpu_custom_call" | custom-call | tf_op jit(solution)/shard_map/reduce/pallas_call | solution.py:171
  15.4 4.7 %update.1 = (f32[32,8192]{1,0:T(8,128)}, f32[32,32]{1,0:T(8,128)}, f32[32,224]{1,0:T(8,128)}, f32[224,8192]{1,0:T(8,128)}) custom-call(f32[256,8192]{1,0:T(8,128)S(1)} %get-tuple-element.7.snap, bf16[64,8192]{1,0:T(8,128)(2,1)S(1)} %get-tuple-element.8.stack, f32[2,16,256]{2,1,0:T(8,128)S(1)} %get-tuple-element.9.total), custom_call_target="tpu_custom_call" | custom-call | tf_op jit(solution)/shard_map/update/pallas_call | solution.py:197

commit v3 on v2

--- a/solution.py
+++ b/solution.py
@@ -8,7 +8,8 @@
 from jax.sharding import PartitionSpec as P
 
 PANEL = 32
-CHUNK = 1024
+LOADS = (2, 2, 2, 2)
+STORES = (1, 1, 1, 1, 1, 1, 1, 1)
 LANES = 128
 BLOCK = 8
 MESH = pl.DeviceIdType.MESH
@@ -17,6 +18,11 @@
 def split(value):
     high = value.astype(jnp.bfloat16)
     return high, (value - high.astype(jnp.float32)).astype(jnp.bfloat16)
+
+
+def spans(width, shares):
+    ends = [width * sum(shares[:i]) // sum(shares) for i in range(len(shares) + 1)]
+    return [pl.ds(low, high - low) for low, high in zip(ends, ends[1:])]
 
 
 def reduce_kernel(chips, x_hbm, snap, stack, total, acc, part, pair_in, slots, full,
@@ -26,13 +32,12 @@
     chip = lax.div(me, 2)
     partner = me + 1 - 2 * core
     cols, width = snap.shape
-    chunks = width // CHUNK
+    loads = spans(width, LOADS)
 
     def load(c):
-        where = pl.ds(pl.multiple_of(c * CHUNK, CHUNK), CHUNK)
-        return pltpu.make_async_copy(x_hbm.at[:, where], snap.at[:, where], load_sem.at[c])
-
-    for c in range(chunks):
+        return pltpu.make_async_copy(x_hbm.at[:, loads[c]], snap.at[:, loads[c]], load_sem.at[c])
+
+    for c in range(len(loads)):
         load(c).start()
 
     barrier = pltpu.get_barrier_semaphore()
@@ -42,16 +47,16 @@
         pl.semaphore_signal(barrier, inc=1, device_id={"rows": peer}, device_id_type=MESH)
 
     acc[...] = jnp.zeros_like(acc)
-    for c in range(chunks):
+    for c in range(len(loads)):
         load(c).wait()
-        where = pl.ds(c * CHUNK, CHUNK)
+        where = loads[c]
         high, low = split(snap[:, where])
         panel = jnp.concatenate([high[:PANEL], low[:PANEL]], axis=0)
         stack[:, where] = panel
         acc[...] += lax.dot_general(
-            jnp.concatenate([high, low], axis=0), panel, (((1,), (1,)), ((), ())),
-            preferred_element_type=jnp.float32)
-    both = acc[:cols] + acc[cols:]
+            high, panel, (((1,), (1,)), ((), ())), preferred_element_type=jnp.float32) + lax.dot_general(
+            low, panel, (((1,), (1,)), ((), ())), preferred_element_type=jnp.float32)
+    both = acc[...]
     gram = (both[:, :PANEL] + both[:, PANEL:]).T
     half = PANEL // 2
     part[0] = gram[:half]
@@ -146,8 +151,7 @@
     weights = jnp.concatenate([lower, -(solved.T)[PANEL:]], axis=0)
     high, low = split(weights)
     coef = jnp.concatenate([high, high, low, low], axis=1)
-    for c in range(width // CHUNK):
-        where = pl.ds(c * CHUNK, CHUNK)
+    for c, where in enumerate(spans(width, STORES)):
         panel = stack[:, where]
         delta = lax.dot_general(
             coef, jnp.concatenate([panel, panel], axis=0), (((1,), (0,)), ((), ())),
@@ -177,12 +181,12 @@
         in_specs=[pl.BlockSpec(memory_space=pltpu.HBM)],
         out_specs=(vmem, vmem, vmem),
         scratch_shapes=[
-            pltpu.VMEM((2 * cols, 2 * PANEL), f32),
+            pltpu.VMEM((cols, 2 * PANEL), f32),
             pltpu.VMEM((2, half, cols), f32),
             pltpu.VMEM((half, cols), f32),
             pltpu.VMEM((chips, half, cols), f32),
             pltpu.VMEM((2, half, cols), f32),
-            pltpu.SemaphoreType.DMA((width // CHUNK,)),
+            pltpu.SemaphoreType.DMA((len(LOADS),)),
             pltpu.SemaphoreType.DMA,
             pltpu.SemaphoreType.DMA,
             pltpu.SemaphoreType.DMA((chips - 1,)),
@@ -207,7 +211,7 @@
             pltpu.VMEM((cols, width), f32),
             pltpu.VMEM((PANEL, PANEL), f32),
             pltpu.VMEM((PANEL, cols - PANEL), f32),
-            pltpu.SemaphoreType.DMA((2 * (width // CHUNK) + 2,)),
+            pltpu.SemaphoreType.DMA((2 * len(STORES) + 2,)),
         ],
         compiler_params=pltpu.CompilerParams(vmem_limit_bytes=32 << 20),
         name="update",

time: 20.3 us -> 20 us (0.985)
  Pallas kernels: 19.5 us -> 19.2 us
    pallas_call x1, Pallas kernels: 14.8 us -> 14.5 us  [local(): pl.pallas_call(functools.partial(reduce_kernel, chips), out_shape=(pltpu....]
where the time goes in v3:
time: 20 us; the launch traced here: 19.8 us
  Pallas kernels  19.2 us (96%)
  between operations  0.64 us (3%)
    pallas_call x1, Pallas kernels, local(): pl.pallas_call(functools.partial(reduce_kernel, chips), out_shape=(pltpu....  14.5 us
    pallas_call x1, Pallas kernels, local(): pl.pallas_call(update_kernel, out_shape=(jax.ShapeDtypeStruct((PANEL, wid...  4.69 us

profile of v3, /device:TPU:0, one launch (start us, length us, event | category | flops | bytes accessed | tf_op | source)
XLA Modules:
  0.0 19.8 jit_solution(18252783084845887369)
XLA Ops:
  0.6 14.5 %reduce.1 = (f32[256,8192]{1,0:T(8,128)S(1)}, bf16[64,8192]{1,0:T(8,128)(2,1)S(1)}, f32[2,16,256]{2,1,0:T(8,128)S(1)}) custom-call(f32[256,8192]{1,0:T(8,128)} %x_hbm.1), custom_call_target="tpu_custom_call" | custom-call | tf_op jit(solution)/shard_map/reduce/pallas_call | solution.py:175
  15.1 4.7 %update.1 = (f32[32,8192]{1,0:T(8,128)}, f32[32,32]{1,0:T(8,128)}, f32[32,224]{1,0:T(8,128)}, f32[224,8192]{1,0:T(8,128)}) custom-call(f32[256,8192]{1,0:T(8,128)S(1)} %get-tuple-element.7.snap, bf16[64,8192]{1,0:T(8,128)(2,1)S(1)} %get-tuple-element.8.stack, f32[2,16,256]{2,1,0:T(8,128)S(1)} %get-tuple-element.9.total), custom_call_target="tpu_custom_call" | custom-call | tf_op jit(solution)/shard_map/update/pallas_call | solution.py:201
